TPU v7x, 32 devices: a whole 2x2x4 slice. The times are simulated.
32 devices in a mesh: atom: 8 (over z, x), aux: 4 (over y, core).
Axes of the slice: x: 2, y: 2, z: 4, core: 2. Of those that a mesh axis runs over, the one named last changes fastest.
Arguments:
- three_index: bfloat16 [128, 32, 128, 128], P('atom', 'aux'), may hold values from -6 to 6
- pair_mask: int32 [128, 8, 8], P('atom'), may hold values 0 or 1
- pair_owner: int32 [128, 1], P('atom'), may hold values from 0 to 7; in each aligned block of 16 rows (0 to 15, 16 to 31, ...) at most 2 rows name the same one
- pair_sub: int32 [128], P('atom'), may hold values from 0 to 3
- pair_nu: int32 [128], P('atom'), may hold values from 0 to 31
- live_count: int32 [8], P('atom'), may hold values from 1 to 16, 96 in all
- coefficients: bfloat16 [4096, 128], P('atom'), may hold values from -0.5 to 0.5
- fit_matrix: bfloat16 [32, 32], P('aux'), as said below
Outputs:
- exchange: float32 [4096, 4096], P('atom', 'aux')
Inputs may be any that keep to these rules, and one draw needn't show every extreme that they name: `pair_owner`: among the 16 slots of one atom index, at most 2 name the same owner, and in every draw some owner is named exactly 2 times by some atom index's slots. The first live_count[a] slots of atom index a are live; some atom index has all 16 slots live. `fit_matrix`: Symmetric.
All inputs are finite; a program needn't handle non-finite values. No bound on the sum of `pair_mask` or of `live_count` on one device may be relied on, other than what follows from the above.
Results may differ from a plain program's by a relative error of at most 0.012.
Values may be sent and summed in bfloat16 or wider, within the bound.
A program may use at most 128 MiB of HBM per device.

v0:
```python
import jax
import jax.numpy as jnp
from jax import lax
from jax.sharding import PartitionSpec as P

CAP = 2


def per_device(
    three_index, pair_mask, pair_owner, pair_sub, pair_nu, live_count, coefficients, fit_matrix
):
    slot_count, aux_here, block_size, _ = three_index.shape
    rows_here, occupied = coefficients.shape
    blocks_here = rows_here // block_size
    atom_count = lax.axis_size("atom")
    aux_total = fit_matrix.shape[1]
    basis_total = rows_here * atom_count
    shell_size = block_size // pair_mask.shape[1]
    whole_orbitals = lax.all_gather(coefficients, "atom", axis=0, tiled=True)
    orbital_blocks = whole_orbitals.reshape(basis_total // block_size, block_size, occupied)[
        pair_nu
    ]
    expanded = jnp.repeat(jnp.repeat(pair_mask, shell_size, 1), shell_size, 2).astype(jnp.bfloat16)
    masked = three_index * expanded[:, None, :, :]
    halfway = jnp.einsum(
        "tpmn,tni->tpim", masked, orbital_blocks, preferred_element_type=jnp.float32
    )
    alive_mask = jnp.arange(slot_count) < live_count[0]
    halfway = jnp.where(alive_mask[:, None, None, None], halfway, 0.0).astype(jnp.bfloat16)
    owners = pair_owner[:, 0]
    owner_hits = (owners[:, None] == jnp.arange(atom_count)[None, :]).astype(jnp.int32)
    rank_within = jnp.sum(jnp.cumsum(owner_hits, 0) * owner_hits, 1) - 1
    placement = owners * CAP + rank_within
    routing = (jnp.arange(atom_count * CAP)[:, None] == placement[None, :]).astype(jnp.bfloat16)
    outgoing = jnp.dot(routing, halfway.reshape(slot_count, -1), preferred_element_type=jnp.float32)
    outgoing = outgoing.astype(jnp.bfloat16).reshape(
        atom_count, CAP, aux_here, occupied, block_size
    )
    sub_codes = jnp.dot(
        routing, (pair_sub + 1).astype(jnp.bfloat16)[:, None], preferred_element_type=jnp.float32
    )
    sub_codes = sub_codes.astype(jnp.bfloat16).reshape(atom_count, CAP)
    arrived, arrived_codes = (
        lax.all_to_all(outgoing, "atom", split_axis=0, concat_axis=0, tiled=True),
        lax.all_to_all(sub_codes, "atom", split_axis=0, concat_axis=0, tiled=True),
    )
    wanted = (jnp.arange(blocks_here) + 1).astype(jnp.float32)
    selector = (arrived_codes.reshape(1, -1).astype(jnp.float32) == wanted[:, None]).astype(
        jnp.bfloat16
    )
    gathered_rows = jnp.einsum(
        "sc,cpib->pisb",
        selector,
        arrived.reshape(atom_count * CAP, aux_here, occupied, block_size),
        preferred_element_type=jnp.float32,
    )
    local_rows = gathered_rows.reshape(aux_here, occupied, rows_here).astype(jnp.bfloat16)
    fitted_sum = jnp.einsum(
        "qp,pir->qir",
        fit_matrix,
        lax.all_gather(local_rows, "aux", axis=0, tiled=True),
        preferred_element_type=jnp.float32,
    )
    fitted = fitted_sum.astype(jnp.bfloat16)
    partial_value = lax.dot_general(
        local_rows,
        lax.all_gather(fitted, "atom", axis=2, tiled=True),
        (((0, 1), (0, 1)), ((), ())),
        preferred_element_type=jnp.float32,
    )
    column_part = lax.psum_scatter(
        partial_value.astype(jnp.bfloat16), "aux", scatter_dimension=1, tiled=True
    ).astype(jnp.float32)
    return column_part * (aux_total * occupied) ** (-0.5)


def solution(mesh):
    in_specs = (
        P("atom", "aux", None, None),
        P("atom", None, None),
        P("atom", None),
        P("atom"),
        P("atom"),
        P("atom"),
        P("atom", None),
        P("aux", None),
    )
    out_specs = P("atom", "aux")
    return jax.shard_map(
        per_device, mesh=mesh, in_specs=in_specs, out_specs=out_specs, check_vma=False
    )
```

profile of v0, /device:TPU:0, one launch (start us, length us, event | category | flops | bytes accessed | tf_op | source)
XLA Modules:
  0.0 409.8 jit_solution(733651022336806653)
XLA Ops:
  6.5 0.0 copy-start
  6.5 0.0 all-gather.4.cloned.1.call-start
  6.5 0.7 all-gather.4.cloned.1.call-update
  7.3 0.7 fusion.25
  8.0 0.8 select_reduce_fusion
  8.9 0.7 add_add_fusion
  9.5 0.8 fusion.23
  10.3 0.7 all_to_all.12
  11.0 7.3 %all-to-all-start.1 = ((bf16[8,1,2]{2,1,0:T(2,128)(2,1)}), bf16[8,1,2]{2,1,0:T(2,128)(2,1)S(1)}, u32[]{:S(2)}, u32[]{:S(2)}) async-start(bf16[8,1,2]{2,1,0:T(2,128)(2,1)} %all_to_all.12), calls=%async_computation.1 | async-start | bytes 8192 | tf_op jit(solution)/shard_map/all_to_all | solution.py:45
  18.9 0.8 convert_element_type.76
  19.7 0.1 copy.17
  19.8 0.2 broadcast_in_dim.30
  20.0 0.2 convert_element_type.77
  20.2 0.1 broadcast_in_dim.31
  20.3 0.3 copy.18
  20.6 0.7 compare_select_fusion
  21.3 31.2 %all-gather.4.cloned.1.call-done = bf16[4096,128]{1,0:T(8,128)(2,1)} async-done(((bf16[512,128]{1,0:T(8,128)(2,1)}), bf16[4096,128]{1,0:T(8,128)(2,1)}) %all-gather.4.cloned.1.call-update) | async-done | bytes 1048592 | tf_op jit(solution)/shard_map/all_gather | solution.py:19
  52.5 1.9 gather_fusion
  54.4 4.1 select_convert_fusion
  58.4 2.5 fusion.12
  61.0 2.7 copy.31
  63.7 0.0 all-to-all-done.1
  63.7 4.5 %all-to-all-start = ((bf16[8,2,8,128,128]{4,3,2,1,0:T(8,128)(2,1)}), bf16[8,2,8,128,128]{4,3,2,1,0:T(8,128)(2,1)}, u32[]{:S(2)}, u32[]{:S(2)}) async-start(bf16[8,2,8,128,128]{4,3,2,1,0:T(8,128)(2,1)} %bitcast.52), calls=%async_computation | async-start | bytes 8388608 | tf_op jit(solution)/shard_map/all_to_all | solution.py:44
  68.3 0.2 all-gather.6.cloned.1.call-start
  68.5 0.1 reshape.65
  68.6 91.4 %all-to-all-done = bf16[8,2,8,128,128]{4,3,2,1,0:T(8,128)(2,1)} async-done(((bf16[8,2,8,128,128]{4,3,2,1,0:T(8,128)(2,1)}), bf16[8,2,8,128,128]{4,3,2,1,0:T(8,128)(2,1)}, u32[]{:S(2)}, u32[]{:S(2)}) %all-to-all-start) | async-done | bytes 4194336 | tf_op jit(solution)/shard_map/all_to_all | solution.py:44
  160.0 6.5 %copy.20 = bf16[8,2,8,128,128]{4,1,0,3,2:T(2,128)(2,1)S(1)} copy(bf16[8,2,8,128,128]{4,3,2,1,0:T(8,128)(2,1)} %all-to-all-done) | data formatting | bytes 8388608 | tf_op jit(solution)/shard_map/all_to_all | solution.py:44
  166.5 0.8 fusion.19
  167.3 1.2 convert_element_type.89
  168.5 0.0 copy-start.1
  168.5 0.0 all-gather.6.cloned.1.call-update
  168.5 0.0 all-gather.8.cloned.1.call-start
  168.6 33.6 %all-gather.6.cloned.1.call-done = bf16[32,128,512]{2,1,0:T(8,128)(2,1)} async-done(((bf16[8,128,512]{2,1,0:T(8,128)(2,1)}), bf16[32,128,512]{2,1,0:T(8,128)(2,1)}) %all-gather.6.cloned.1.call-update) | async-done | bytes 4194320 | tf_op jit(solution)/shard_map/all_gather | solution.py:61
  202.2 0.0 copy-done
  202.2 5.6 %fusion.20 = bf16[8,128,512]{2,0,1:T(8,128)(2,1)} fusion(bf16[32,128,512]{2,1,0:T(8,128)(2,1)} %all-gather.6.cloned.1.call-done, bf16[8,32]{1,0:T(8,128)(2,1)S(1)} %copy-done), kind=kOutput, calls=%fused_computation.18 | convolution fusion | flops 34078720 | bytes 5243392 | tf_op jit(solution)/shard_map/qp,pir->qir/dot_general | solution.py:58
  207.8 0.0 all-gather.8.cloned.1.call-update
  207.8 0.3 reduce-scatter.2.cloned.1.call-start
  208.1 124.8 %all-gather.8.cloned.1.call-done = bf16[8,128,4096]{2,0,1:T(8,128)(2,1)} async-done(((bf16[8,128,512]{2,0,1:T(8,128)(2,1)}), bf16[8,128,4096]{2,0,1:T(8,128)(2,1)}) %all-gather.8.cloned.1.call-update) | async-done | bytes 8388624 | tf_op jit(solution)/shard_map/all_gather | solution.py:67
  332.9 0.0 copy-done.1
  332.9 24.8 %bitcast_convert_fusion = bf16[512,4096]{1,0:T(8,128)(2,1)} fusion(bf16[8,128,512]{2,1,0:T(8,128)(2,1)S(1)} %copy-done.1, bf16[8,128,4096]{2,0,1:T(8,128)(2,1)} %all-gather.8.cloned.1.call-done), kind=kOutput, calls=%fused_computation.2 | convolution fusion | flops 4297064448 | bytes 13631488 | tf_op jit(solution)/shard_map/dot_general | solution.py:65
  357.7 0.0 reduce-scatter.2.cloned.1.call-update
  357.7 42.8 %reduce-scatter.2.cloned.1.call-done = bf16[512,1024]{1,0:T(8,128)(2,1)} async-done(((bf16[512,4096]{1,0:T(8,128)(2,1)}), bf16[512,1024]{1,0:T(8,128)(2,1)}) %reduce-scatter.2.cloned.1.call-update) | async-done | bytes 1048592 | tf_op jit(solution)/shard_map/reduce_scatter | solution.py:71
  400.5 2.8 convert_multiply_fusion
  (5 shorter events, 0.1 us)
Async XLA Ops:
  6.5 195.6 %copy-start = (bf16[8,32]{1,0:T(8,128)(2,1)S(1)}, bf16[8,32]{1,0:T(8,128)(2,1)}, u32[]{:S(2)}) copy-start(bf16[8,32]{1,0:T(8,128)(2,1)} %param.15) | copy-start | bytes 1540
  6.5 46.0 %all-gather.4.cloned.1.call-start = ((), (), s32[]{:S(2)}) async-start(), calls=%async_computation.3 | async-start | bytes 1179648 | tf_op jit(solution)/shard_map/all_gather | solution.py:19
  11.0 52.7 %all-to-all-start.1 = ((bf16[8,1,2]{2,1,0:T(2,128)(2,1)}), bf16[8,1,2]{2,1,0:T(2,128)(2,1)S(1)}, u32[]{:S(2)}, u32[]{:S(2)}) async-start(bf16[8,1,2]{2,1,0:T(2,128)(2,1)} %all_to_all.12), calls=%async_computation.1 | async-start | bytes 8192 | tf_op jit(solution)/shard_map/all_to_all | solution.py:45
  63.7 96.3 %all-to-all-start = ((bf16[8,2,8,128,128]{4,3,2,1,0:T(8,128)(2,1)}), bf16[8,2,8,128,128]{4,3,2,1,0:T(8,128)(2,1)}, u32[]{:S(2)}, u32[]{:S(2)}) async-start(bf16[8,2,8,128,128]{4,3,2,1,0:T(8,128)(2,1)} %bitcast.52), calls=%async_computation | async-start | bytes 8388608 | tf_op jit(solution)/shard_map/all_to_all | solution.py:44
  68.3 133.9 %all-gather.6.cloned.1.call-start = ((), (), s32[]{:S(2)}) async-start(), calls=%async_computation.4 | async-start | bytes 5242880 | tf_op jit(solution)/shard_map/all_gather | solution.py:61
  168.5 164.4 %copy-start.1 = (bf16[8,128,512]{2,1,0:T(8,128)(2,1)S(1)}, bf16[8,128,512]{2,1,0:T(8,128)(2,1)}, u32[]{:S(2)}) copy-start(bf16[8,128,512]{2,1,0:T(8,128)(2,1)} %convert_element_type.89) | copy-start | bytes 3145732
  168.5 164.4 %all-gather.8.cloned.1.call-start = ((), (), s32[]{:S(2)}) async-start(), calls=%async_computation.5 | async-start | bytes 9437184 | tf_op jit(solution)/shard_map/all_gather | solution.py:67
  207.8 192.7 %reduce-scatter.2.cloned.1.call-start = ((), (), s32[]{:S(2)}) async-start(), calls=%async_computation.6 | async-start | bytes 5242880 | tf_op jit(solution)/shard_map/reduce_scatter | solution.py:71
Sparse Core Ops, SparseCore 0:
  9.5 42.9 all-gather.3
  168.7 33.4 all-gather.5
  207.9 124.9 all-gather.7
  357.8 42.5 reduce-scatter.1
where the time goes:
time: 410 us
  waiting for transfers between devices  325 us (79%)
  matrix products  38.5 us (9%)
  local copies, waits for them, and re-layouts  14 us (3%)
  between operations  13.9 us (3%)
  starting transfers between devices  12.4 us (3%)
  other arithmetic  6.54 us (2%)
    all_gather x1, waiting for transfers between devices, per_device(): lax.all_gather(fitted, 'atom', axis=2, tiled=True)  125 us
    all_to_all x1, waiting for transfers between devices, per_device(): lax.all_to_all(outgoing, 'atom', split_axis=0, concat_axis=0, tiled=True)  91.4 us
    reduce_scatter x1, waiting for transfers between devices, per_device(): lax.psum_scatter(partial_value.astype(jnp.bfloat16), 'aux', scatter_dimen...  42.8 us
    all_gather x1, waiting for transfers between devices, per_device(): lax.all_gather(local_rows, 'aux', axis=0, tiled=True)  33.6 us
    all_gather x1, waiting for transfers between devices, per_device(): whole_orbitals = lax.all_gather(coefficients, 'atom', axis=0, tiled=True)  31.2 us
    dot_general x1, matrix products, per_device(): lax.dot_general(local_rows, lax.all_gather(fitted, 'atom', axis=2, tiled=...  24.8 us
  transfers between devices with their start and end apart: 6, of which 5 were waited for; matrix products, arithmetic and copies ran while one was open for 4% of the time, Pallas kernels for 0%

commit v1 on v0

--- a/solution.py
+++ b/solution.py
@@ -55,12 +55,37 @@
         preferred_element_type=jnp.float32,
     )
     local_rows = gathered_rows.reshape(aux_here, occupied, rows_here).astype(jnp.bfloat16)
+    length, index, rows = (lax.axis_size("aux"), lax.axis_index("aux"), local_rows.shape[0])
+    right = [(i, (i + 1) % length) for i in range(length)]
+    left = [(i, (i - 1) % length) for i in range(length)]
+    half = length // 2
+    from_left = from_right = local_rows
     fitted_sum = jnp.einsum(
         "qp,pir->qir",
-        fit_matrix,
-        lax.all_gather(local_rows, "aux", axis=0, tiled=True),
+        lax.dynamic_slice_in_dim(fit_matrix, index * rows, local_rows.shape[0], axis=1),
+        local_rows,
         preferred_element_type=jnp.float32,
     )
+    for step in range(1, half + 1):
+        from_left = lax.ppermute(from_left, "aux", right)
+        if step < length - half:
+            from_right = lax.ppermute(from_right, "aux", left)
+            fitted_sum = fitted_sum + jnp.einsum(
+                "qp,pir->qir",
+                lax.dynamic_slice_in_dim(
+                    fit_matrix, (index + step) % length * rows, from_right.shape[0], axis=1
+                ),
+                from_right,
+                preferred_element_type=jnp.float32,
+            )
+        fitted_sum = fitted_sum + jnp.einsum(
+            "qp,pir->qir",
+            lax.dynamic_slice_in_dim(
+                fit_matrix, (index - step) % length * rows, from_left.shape[0], axis=1
+            ),
+            from_left,
+            preferred_element_type=jnp.float32,
+        )
     fitted = fitted_sum.astype(jnp.bfloat16)
     partial_value = lax.dot_general(
         local_rows,

time: 410 us -> 413 us (level)
    ppermute x0 -> x3, waiting for transfers between devices: none -> 34.6 us  [the longest x2 34.6 us: per_device(): from_left = lax.ppermute(from_left, 'aux', right)]
    all_gather x1 -> x0, waiting for transfers between devices: 33.6 us -> none  [per_device(): lax.all_gather(local_rows, 'aux', axis=0, tiled=True)]
  transfers between devices with their start and end apart: 6 -> 8, of which waited for: 5 -> 6; matrix products, arithmetic and copies ran while one was open for 4% -> 4% of each run, Pallas kernels for 0% -> 0%
where the time goes in v1:
time: 413 us; the launch traced here: 412 us
  waiting for transfers between devices  325 us (79%)
  matrix products  37.4 us (9%)
  local copies, waits for them, and re-layouts  14.8 us (4%)
  starting transfers between devices  14.2 us (3%)
  between operations  13.9 us (3%)
  other arithmetic  6.54 us (2%)
    all_gather x1, waiting for transfers between devices, per_device(): lax.all_gather(fitted, 'atom', axis=2, tiled=True)  125 us
    all_to_all x1, waiting for transfers between devices, per_device(): lax.all_to_all(outgoing, 'atom', split_axis=0, concat_axis=0, tiled=True)  91.4 us
    reduce_scatter x1, waiting for transfers between devices, per_device(): lax.psum_scatter(partial_value.astype(jnp.bfloat16), 'aux', scatter_dimen...  42.7 us
    ppermute x2, waiting for transfers between devices, per_device(): from_left = lax.ppermute(from_left, 'aux', right)  34.6 us
    all_gather x1, waiting for transfers between devices, per_device(): whole_orbitals = lax.all_gather(coefficients, 'atom', axis=0, tiled=True)  31.2 us
    dot_general x1, matrix products, per_device(): lax.dot_general(local_rows, lax.all_gather(fitted, 'atom', axis=2, tiled=...  24.8 us
  transfers between devices with their start and end apart: 8, of which 6 were waited for; matrix products, arithmetic and copies ran while one was open for 4% of the time, Pallas kernels for 0%

profile of v1, /device:TPU:0, one launch (start us, length us, event | category | flops | bytes accessed | tf_op | source)
XLA Modules:
  0.0 412.2 jit_solution(9965074642656926662)
XLA Ops:
  6.5 0.0 copy-start
  6.5 0.0 all-gather.3.cloned.1.call-start
  6.5 0.7 all-gather.3.cloned.1.call-update
  7.3 0.7 fusion.17
  8.0 0.8 select_reduce_fusion
  8.9 0.7 add_add_fusion
  9.5 0.8 fusion.15
  10.3 0.7 all_to_all.12
  11.0 7.3 %all-to-all-start.1 = ((bf16[8,1,2]{2,1,0:T(2,128)(2,1)}), bf16[8,1,2]{2,1,0:T(2,128)(2,1)S(1)}, u32[]{:S(2)}, u32[]{:S(2)}) async-start(bf16[8,1,2]{2,1,0:T(2,128)(2,1)} %all_to_all.12), calls=%async_computation.1 | async-start | bytes 8192 | tf_op jit(solution)/shard_map/all_to_all | solution.py:45
  18.9 0.8 convert_element_type.73
  19.7 0.1 copy.17
  19.8 0.2 broadcast_in_dim.30
  20.0 0.2 convert_element_type.74
  20.2 0.1 broadcast_in_dim.31
  20.3 0.3 copy.18
  20.6 0.7 compare_select_fusion
  21.3 31.2 %all-gather.3.cloned.1.call-done = bf16[4096,128]{1,0:T(8,128)(2,1)} async-done(((bf16[512,128]{1,0:T(8,128)(2,1)}), bf16[4096,128]{1,0:T(8,128)(2,1)}) %all-gather.3.cloned.1.call-update) | async-done | bytes 1048592 | tf_op jit(solution)/shard_map/all_gather | solution.py:19
  52.5 1.9 gather_fusion
  54.4 4.1 select_convert_fusion
  58.4 2.5 fusion.10
  61.0 2.8 copy.33
  63.7 0.0 all-to-all-done.1
  63.7 4.5 %all-to-all-start = ((bf16[8,2,8,128,128]{4,3,2,1,0:T(8,128)(2,1)}), bf16[8,2,8,128,128]{4,3,2,1,0:T(8,128)(2,1)}, u32[]{:S(2)}, u32[]{:S(2)}) async-start(bf16[8,2,8,128,128]{4,3,2,1,0:T(8,128)(2,1)} %bitcast.62), calls=%async_computation | async-start | bytes 8388608 | tf_op jit(solution)/shard_map/all_to_all | solution.py:44
  68.3 0.2 all-gather.5.cloned.1.call-start
  68.5 0.1 reshape.65
  68.6 91.4 %all-to-all-done = bf16[8,2,8,128,128]{4,3,2,1,0:T(8,128)(2,1)} async-done(((bf16[8,2,8,128,128]{4,3,2,1,0:T(8,128)(2,1)}), bf16[8,2,8,128,128]{4,3,2,1,0:T(8,128)(2,1)}, u32[]{:S(2)}, u32[]{:S(2)}) %all-to-all-start) | async-done | bytes 4194336 | tf_op jit(solution)/shard_map/all_to_all | solution.py:44
  160.0 6.5 %copy.20 = bf16[8,2,8,128,128]{4,1,0,3,2:T(2,128)(2,1)S(1)} copy(bf16[8,2,8,128,128]{4,3,2,1,0:T(8,128)(2,1)} %all-to-all-done) | data formatting | bytes 8388608 | tf_op jit(solution)/shard_map/all_to_all | solution.py:44
  166.5 0.8 fusion.14
  167.3 0.4 convert_element_type.86
  167.7 1.5 copy.22
  169.3 0.0 collective-permute-start.1
  169.3 1.7 collective-permute-start
  171.0 22.2 %collective-permute-done.1 = bf16[8,128,512]{2,0,1:T(8,128)(2,1)S(1)} collective-permute-done((bf16[8,128,512]{2,0,1:T(8,128)(2,1)}, bf16[8,128,512]{2,0,1:T(8,128)(2,1)S(1)}, u32[]{:S(2)}, u32[]{:S(2)}) %collective-permute-start.1) | collective-permute-done | bytes 1048608 | tf_op jit(solution)/shard_map/ppermute | solution.py:70
  193.2 0.1 collective-permute-start.2
  193.3 0.0 copy-done
  193.3 0.7 fusion.25
  194.1 0.5 fusion.21
  194.6 0.0 collective-permute-done
  194.6 0.5 fusion.23
  195.1 12.5 %collective-permute-done.2 = bf16[8,128,512]{2,0,1:T(8,128)(2,1)} collective-permute-done((bf16[8,128,512]{2,0,1:T(8,128)(2,1)S(1)}, bf16[8,128,512]{2,0,1:T(8,128)(2,1)}, u32[]{:S(2)}, u32[]{:S(2)}) %collective-permute-start.2) | collective-permute-done | bytes 1048608 | tf_op jit(solution)/shard_map/ppermute | solution.py:70
  207.5 2.8 add_convert_fusion
  210.3 0.0 all-gather.5.cloned.1.call-update
  210.3 0.3 reduce-scatter.2.cloned.1.call-start
  210.6 124.8 %all-gather.5.cloned.1.call-done = bf16[8,128,4096]{2,0,1:T(8,128)(2,1)} async-done(((bf16[8,128,512]{2,0,1:T(8,128)(2,1)}), bf16[8,128,4096]{2,0,1:T(8,128)(2,1)}) %all-gather.5.cloned.1.call-update) | async-done | bytes 8388624 | tf_op jit(solution)/shard_map/all_gather | solution.py:92
  335.4 24.8 %bitcast_convert_fusion = bf16[512,4096]{1,0:T(8,128)(2,1)} fusion(bf16[8,128,512]{2,1,0:T(8,128)(2,1)S(1)} %convert_element_type.86, bf16[8,128,4096]{2,0,1:T(8,128)(2,1)} %all-gather.5.cloned.1.call-done), kind=kOutput, calls=%fused_computation.2 | convolution fusion | flops 4297064448 | bytes 13631488 | tf_op jit(solution)/shard_map/dot_general | solution.py:90
  360.1 0.0 reduce-scatter.2.cloned.1.call-update
  360.2 42.7 %reduce-scatter.2.cloned.1.call-done = bf16[512,1024]{1,0:T(8,128)(2,1)} async-done(((bf16[512,4096]{1,0:T(8,128)(2,1)}), bf16[512,1024]{1,0:T(8,128)(2,1)}) %reduce-scatter.2.cloned.1.call-update) | async-done | bytes 1048592 | tf_op jit(solution)/shard_map/reduce_scatter | solution.py:96
  402.9 2.8 convert_multiply_fusion
  (5 shorter events, 0.1 us)
Async XLA Ops:
  6.5 186.8 %copy-start = (bf16[8,32]{1,0:T(8,128)(2,1)S(1)}, bf16[8,32]{1,0:T(8,128)(2,1)}, u32[]{:S(2)}) copy-start(bf16[8,32]{1,0:T(8,128)(2,1)} %param.15) | copy-start | bytes 1540
  6.5 46.0 %all-gather.3.cloned.1.call-start = ((), (), s32[]{:S(2)}) async-start(), calls=%async_computation.3 | async-start | bytes 1179648 | tf_op jit(solution)/shard_map/all_gather | solution.py:19
  11.0 52.7 %all-to-all-start.1 = ((bf16[8,1,2]{2,1,0:T(2,128)(2,1)}), bf16[8,1,2]{2,1,0:T(2,128)(2,1)S(1)}, u32[]{:S(2)}, u32[]{:S(2)}) async-start(bf16[8,1,2]{2,1,0:T(2,128)(2,1)} %all_to_all.12), calls=%async_computation.1 | async-start | bytes 8192 | tf_op jit(solution)/shard_map/all_to_all | solution.py:45
  63.7 96.3 %all-to-all-start = ((bf16[8,2,8,128,128]{4,3,2,1,0:T(8,128)(2,1)}), bf16[8,2,8,128,128]{4,3,2,1,0:T(8,128)(2,1)}, u32[]{:S(2)}, u32[]{:S(2)}) async-start(bf16[8,2,8,128,128]{4,3,2,1,0:T(8,128)(2,1)} %bitcast.62), calls=%async_computation | async-start | bytes 8388608 | tf_op jit(solution)/shard_map/all_to_all | solution.py:44
  68.3 267.1 %all-gather.5.cloned.1.call-start = ((), (), s32[]{:S(2)}) async-start(), calls=%async_computation.4 | async-start | bytes 9437184 | tf_op jit(solution)/shard_map/all_gather | solution.py:92
  169.3 23.9 %collective-permute-start.1 = (bf16[8,128,512]{2,0,1:T(8,128)(2,1)}, bf16[8,128,512]{2,0,1:T(8,128)(2,1)S(1)}, u32[]{:S(2)}, u32[]{:S(2)}) collective-permute-start(bf16[8,128,512]{2,0,1:T(8,128)(2,1)} %copy.22), channel_id=1, source_target_pairs={{0,1},{1,2},{2,3},{3,0},{4,5},{5,6},{6,7},{7,4},{8,9},{9,10},{10,1... | collective-permute-start | bytes 3145736 | tf_op jit(solution)/shard_map/ppermute | solution.py:70
  169.3 25.3 %collective-permute-start = (bf16[8,128,512]{2,0,1:T(8,128)(2,1)}, bf16[8,128,512]{2,0,1:T(8,128)(2,1)S(1)}, u32[]{:S(2)}, u32[]{:S(2)}) collective-permute-start(bf16[8,128,512]{2,0,1:T(8,128)(2,1)} %copy.22), channel_id=1, source_target_pairs={{0,3},{1,0},{2,1},{3,2},{4,7},{5,4},{6,5},{7,6},{8,11},{9,8},{10,9... | collective-permute-start | bytes 3145736 | tf_op jit(solution)/shard_map/ppermute | solution.py:72
  193.2 14.3 %collective-permute-start.2 = (bf16[8,128,512]{2,0,1:T(8,128)(2,1)S(1)}, bf16[8,128,512]{2,0,1:T(8,128)(2,1)}, u32[]{:S(2)}, u32[]{:S(2)}) collective-permute-start(bf16[8,128,512]{2,0,1:T(8,128)(2,1)S(1)} %collective-permute-done.1), channel_id=1, source_target_pairs={{0,1},{1,2},{2,3},{3,0},{4,5},{5,6},{6,7},{7,4},{8,9},{9,10},{10,1... | collective-permute-start | bytes 3145736 | tf_op jit(solution)/shard_map/ppermute | solution.py:70
  210.3 192.6 %reduce-scatter.2.cloned.1.call-start = ((), (), s32[]{:S(2)}) async-start(), calls=%async_computation.5 | async-start | bytes 5242880 | tf_op jit(solution)/shard_map/reduce_scatter | solution.py:96
Sparse Core Ops, SparseCore 0:
  9.5 42.9 all-gather.2
  210.4 124.8 all-gather.4
  360.3 42.5 reduce-scatter.1
